TPU v7x, 256 devices: a whole 4x4x8 slice. The times are simulated.
256 devices in a mesh: row: 16 (over x_lo, y, core), col: 16 (over x_hi, z).
Axes of the slice: x: 4 (x_hi: 2, x_lo: 2; x = x_hi * 2 + x_lo), y: 4, z: 8, core: 2. Of those that a mesh axis runs over, the one named last changes fastest.
Arguments:
- node_features: bfloat16 [65536, 256], P(('row', 'col')), may hold values from -6 to 6
- tile_values: bfloat16 [16, 16, 128, 128, 128], P('row', 'col'), may hold values from -0.09375 to 0.09375
- tile_coords: int32 [16, 16, 128, 2], P('row', 'col'), may hold values from 0 to 31, as said below
- tile_counts: int32 [16, 16], P('row', 'col'), may hold values from 32 to 128, as said below
- first_weight: bfloat16 [256, 256], replicated, may hold values from -0.375 to 0.375
- second_weight: bfloat16 [256, 128], replicated, may hold values from -0.375 to 0.375
- out_grad: bfloat16 [65536, 128], P(('row', 'col')), may hold values from -6 to 6
Outputs:
- output: bfloat16 [65536, 128], P(('row', 'col'))
- first_grad: float32 [256, 256], replicated
- second_grad: float32 [256, 128], replicated
Inputs may be any that keep to these rules, and one draw needn't show every extreme that they name: `tile_counts`: each grid cell uses at least 32 slots; at least one grid cell uses all 128 in every draw. `tile_coords`: the first entry is a tile row below 32, the second a tile column below 32; within one grid cell no two slots share a position.
All inputs are finite; a program needn't handle non-finite values.
Results may differ from a plain program's by a relative error of at most 0.005.
Values may be sent and summed in bfloat16 or wider, within the bound.
A program may use at most 64 MiB of HBM per device.

v0:
```python
import math
import jax
import jax.numpy as jnp
from jax import lax
from jax.sharding import PartitionSpec as P

HIGHEST = lax.Precision.HIGHEST


def tile_sum(tile_block, dest_index, source_index, live_slots, source, dest_tiles, flipped):
    slot_count = tile_block.shape[0]
    group_size = math.gcd(slot_count, 32)
    round_count = slot_count // group_size
    edge_size = tile_block.shape[1]
    width_size = source.shape[-1]
    grouped_tiles = tile_block.reshape(round_count, group_size, edge_size, edge_size)
    grouped_dest = dest_index.reshape(round_count, group_size)
    grouped_source = source_index.reshape(round_count, group_size)
    grouped_live = live_slots.reshape(round_count, group_size)
    target_ids = jnp.arange(dest_tiles, dtype=jnp.int32)
    einsum_form = "tba,tbw->taw" if flipped else "tab,tbw->taw"

    def add_group(running, pieces):
        group_tiles, group_dest, group_source, group_live = pieces
        picked = jnp.take(source, group_source, axis=0)
        products = jnp.einsum(einsum_form, group_tiles, picked, preferred_element_type=jnp.float32)
        select = ((group_dest[:, None] == target_ids[None, :]) & group_live[:, None]).astype(
            jnp.float32
        )
        running = running + jnp.einsum("tr,taw->raw", select, products, precision=HIGHEST)
        return (running, None)

    start_sum = jnp.zeros((dest_tiles, edge_size, width_size), jnp.float32)
    running, unused = lax.scan(
        add_group, start_sum, (grouped_tiles, grouped_dest, grouped_source, grouped_live)
    )
    return running.reshape(dest_tiles * edge_size, width_size)


def on_device(
    node_features, tile_values, tile_coords, tile_counts, first_weight, second_weight, out_grad
):
    node_rows = node_features.shape[0]
    edge_size = tile_values.shape[-1]
    slot_count = tile_values.shape[2]
    grid_rows = lax.axis_size("row")
    grid_cols = lax.axis_size("col")
    row_tiles = grid_rows * node_rows // edge_size
    col_tiles = grid_cols * node_rows // edge_size
    tile_block = tile_values.reshape(slot_count, edge_size, edge_size)
    flat_coords = tile_coords.reshape(slot_count, 2)
    tile_row = flat_coords[:, 0]
    tile_col = flat_coords[:, 1]
    live_slots = jnp.arange(slot_count, dtype=jnp.int32) < tile_counts.reshape(())
    gathered_x = lax.all_gather(node_features, "col", axis=0, tiled=True)
    feature_part = tile_sum(
        tile_block,
        tile_row,
        tile_col,
        live_slots,
        gathered_x.reshape(col_tiles, edge_size, -1),
        row_tiles,
        False,
    )
    first_mean = lax.psum_scatter(feature_part, "row", scatter_dimension=0, tiled=True)
    first_pre = jnp.dot(first_mean, first_weight.astype(jnp.float32), precision=HIGHEST)
    hidden_act = jax.nn.silu(first_pre).astype(jnp.bfloat16)
    second_wide = second_weight.astype(jnp.float32)
    gathered_h = lax.all_gather(hidden_act, "col", axis=0, tiled=True)
    hidden_part = tile_sum(
        tile_block,
        tile_row,
        tile_col,
        live_slots,
        gathered_h.reshape(col_tiles, edge_size, -1),
        row_tiles,
        False,
    )
    second_mean = lax.psum_scatter(hidden_part, "row", scatter_dimension=0, tiled=True)
    logit_rows = jnp.dot(second_mean, second_wide, precision=HIGHEST)
    output = logit_rows.astype(jnp.bfloat16)
    gathered_g = lax.all_gather(out_grad, "row", axis=0, tiled=True)
    grad_part = tile_sum(
        tile_block,
        tile_col,
        tile_row,
        live_slots,
        gathered_g.reshape(row_tiles, edge_size, -1),
        col_tiles,
        True,
    )
    back_sum = lax.psum_scatter(grad_part, "col", scatter_dimension=0, tiled=True)
    scale = 1.0 / math.sqrt(node_rows * grid_rows * grid_cols)
    second_local = jnp.dot(hidden_act.astype(jnp.float32).T, back_sum, precision=HIGHEST) * scale
    hidden_grad = jnp.dot(back_sum, second_wide.T, precision=HIGHEST)
    sigma = jax.nn.sigmoid(first_pre)
    pre_grad = hidden_grad * (sigma * (1.0 + first_pre * (1.0 - sigma)))
    second_grad = lax.psum(second_local, ("row", "col"))
    first_local = jnp.dot(first_mean.T, pre_grad, precision=HIGHEST) * scale
    first_grad = lax.psum(first_local, ("row", "col"))
    return (output, first_grad, second_grad)


def solution(mesh):
    return jax.shard_map(
        on_device,
        mesh=mesh,
        in_specs=(
            P(("row", "col"), None),
            P("row", "col", None, None, None),
            P("row", "col", None, None),
            P("row", "col"),
            P(),
            P(),
            P(("row", "col"), None),
        ),
        out_specs=(P(("row", "col"), None), P(), P()),
        check_vma=False,
    )
```

profile of v0, /device:TPU:1, one launch (start us, length us, event | category | flops | bytes accessed | tf_op | source)
XLA Modules:
  0.0 898.8 jit_solution(9143985936863349914)
XLA Ops:
  9.6 86.8 %all-gather.4.cloned.1.call-done = bf16[4096,256]{1,0:T(8,128)(2,1)} async-done(((bf16[256,256]{1,0:T(8,128)(2,1)}), bf16[4096,256]{1,0:T(8,128)(2,1)}) %all-gather.4.cloned.1.call-update) | async-done | bytes 2097168 | tf_op jit(solution)/shard_map/all_gather | solution.py:55
  96.3 64.7 %while.33 = (s32[]{:T(128)}, f32[32,128,256]{2,0,1:T(8,128)}, s32[4,32]{1,0:T(4,128)S(1)}, pred[4,32]{1,0:T(4,128)(4,1)S(1)}, bf16[4,32,128,128]{3,2,1,0:T(8,128...) while((s32[]{:T(128)}, f32[32,128,256]{2,0,1:T(8,128)}, ...), condition=%wide.region_1.3_spmd.clone, body=%wide.region_0.2_spmd.clone.sunk | while | flops 674237632 | bytes 24123028 | solution.py:34
  102.6 8.9 select_add_fusion.6
  117.9 10.2 %select_add_fusion.6 = f32[32,128,256]{2,0,1:T(8,128)} fusion(f32[32,128,256]{2,0,1:T(8,128)} %get-tuple-element.410, f32[32,128,256]{2,1,0:T(8,128)} %fusion.96, pred[]{:T(512)S(6)} %compare.9, s32[32]{0:T(128)S(1)} %fusion.97, pred[32]{0:T(512)(128)(4,1)S(1)} %dynamic-slice_bitcast_fusion.6), kind=kOutput, calls=%fused_computation.33.clone.1 | convolution fusion | flops 404752384 | bytes 12583073 | tf_op jit(solution)/shard_map/while/body/eval_jaxpr/tr,taw->raw/dot_general | solution.py:30
  134.4 10.2 %select_add_fusion.6 = f32[32,128,256]{2,0,1:T(8,128)} fusion(f32[32,128,256]{2,0,1:T(8,128)} %get-tuple-element.410, f32[32,128,256]{2,1,0:T(8,128)} %fusion.96, pred[]{:T(512)S(6)} %compare.9, s32[32]{0:T(128)S(1)} %fusion.97, pred[32]{0:T(512)(128)(4,1)S(1)} %dynamic-slice_bitcast_fusion.6), kind=kOutput, calls=%fused_computation.33.clone.1 | convolution fusion | flops 404752384 | bytes 12583073 | tf_op jit(solution)/shard_map/while/body/eval_jaxpr/tr,taw->raw/dot_general | solution.py:30
  150.9 10.2 %select_add_fusion.6 = f32[32,128,256]{2,0,1:T(8,128)} fusion(f32[32,128,256]{2,0,1:T(8,128)} %get-tuple-element.410, f32[32,128,256]{2,1,0:T(8,128)} %fusion.96, pred[]{:T(512)S(6)} %compare.9, s32[32]{0:T(128)S(1)} %fusion.97, pred[32]{0:T(512)(128)(4,1)S(1)} %dynamic-slice_bitcast_fusion.6), kind=kOutput, calls=%fused_computation.33.clone.1 | convolution fusion | flops 404752384 | bytes 12583073 | tf_op jit(solution)/shard_map/while/body/eval_jaxpr/tr,taw->raw/dot_general | solution.py:30
  161.0 6.6 copy.10
  168.5 65.5 %reduce-scatter.4.cloned.1.call-done = f32[256,256]{1,0:T(8,128)} async-done(((f32[4096,256]{1,0:T(8,128)}), f32[256,256]{1,0:T(8,128)}) %reduce-scatter.4.cloned.1.call-update) | async-done | bytes 262160 | tf_op jit(solution)/shard_map/reduce_scatter | solution.py:65
  236.2 37.0 %all-gather.8.cloned.1.call-done = bf16[4096,128]{1,0:T(8,128)(2,1)} async-done(((bf16[256,128]{1,0:T(8,128)(2,1)}), bf16[4096,128]{1,0:T(8,128)(2,1)}) %all-gather.8.cloned.1.call-update) | async-done | bytes 1048592 | tf_op jit(solution)/shard_map/all_gather | solution.py:82
  273.2 35.7 %while.35 = (s32[]{:T(128)}, f32[32,128,128]{2,0,1:T(8,128)}, s32[4,32]{1,0:T(4,128)S(1)}, pred[4,32]{1,0:T(4,128)(4,1)S(1)}, bf16[4,32,128,128]{3,2,1,0:T(8,128...) while((s32[]{:T(128)}, f32[32,128,128]{2,0,1:T(8,128)}, ...), condition=%wide.region_7.9_spmd.clone, body=%wide.region_6.8_spmd.clone.sunk | while | flops 337120544 | bytes 12588823 | solution.py:34
  284.7 5.4 select_add_fusion.8
  294.0 5.5 select_add_fusion.8
  303.4 5.5 select_add_fusion.8
  308.8 4.2 copy.12
  313.0 44.8 %all-gather.6.cloned.1.call-done = bf16[4096,256]{1,0:T(8,128)(2,1)} async-done(((bf16[256,256]{1,0:T(8,128)(2,1)}), bf16[4096,256]{1,0:T(8,128)(2,1)}) %all-gather.6.cloned.1.call-update) | async-done | bytes 2097168 | tf_op jit(solution)/shard_map/all_gather | solution.py:69
  357.8 65.0 %while.34 = (s32[]{:T(128)}, f32[32,128,256]{2,0,1:T(8,128)}, s32[4,32]{1,0:T(4,128)S(1)}, pred[4,32]{1,0:T(4,128)(4,1)S(1)}, bf16[4,32,128,128]{3,2,1,0:T(8,128...) while((s32[]{:T(128)}, f32[32,128,256]{2,0,1:T(8,128)}, ...), condition=%wide.region_4.6_spmd.clone, body=%wide.region_3.5_spmd.clone.sunk | while | flops 674237632 | bytes 24123028 | solution.py:34
  364.1 8.9 select_add_fusion.7
  379.4 10.2 %select_add_fusion.7 = f32[32,128,256]{2,0,1:T(8,128)} fusion(f32[32,128,256]{2,0,1:T(8,128)} %get-tuple-element.437, f32[32,128,256]{2,1,0:T(8,128)} %fusion.102, pred[]{:T(512)S(6)} %compare.10, s32[32]{0:T(128)S(1)} %fusion.103, pred[32]{0:T(512)(128)(4,1)S(1)} %dynamic-slice_bitcast_fusion.7), kind=kOutput, calls=%fused_computation.57.clone.1 | convolution fusion | flops 404752384 | bytes 12583073 | tf_op jit(solution)/shard_map/while/body/eval_jaxpr/tr,taw->raw/dot_general | solution.py:30
  396.0 10.3 %select_add_fusion.7 = f32[32,128,256]{2,0,1:T(8,128)} fusion(f32[32,128,256]{2,0,1:T(8,128)} %get-tuple-element.437, f32[32,128,256]{2,1,0:T(8,128)} %fusion.102, pred[]{:T(512)S(6)} %compare.10, s32[32]{0:T(128)S(1)} %fusion.103, pred[32]{0:T(512)(128)(4,1)S(1)} %dynamic-slice_bitcast_fusion.7), kind=kOutput, calls=%fused_computation.57.clone.1 | convolution fusion | flops 404752384 | bytes 12583073 | tf_op jit(solution)/shard_map/while/body/eval_jaxpr/tr,taw->raw/dot_general | solution.py:30
  412.6 10.2 %select_add_fusion.7 = f32[32,128,256]{2,0,1:T(8,128)} fusion(f32[32,128,256]{2,0,1:T(8,128)} %get-tuple-element.437, f32[32,128,256]{2,1,0:T(8,128)} %fusion.102, pred[]{:T(512)S(6)} %compare.10, s32[32]{0:T(128)S(1)} %fusion.103, pred[32]{0:T(512)(128)(4,1)S(1)} %dynamic-slice_bitcast_fusion.7), kind=kOutput, calls=%fused_computation.57.clone.1 | convolution fusion | flops 404752384 | bytes 12583073 | tf_op jit(solution)/shard_map/while/body/eval_jaxpr/tr,taw->raw/dot_general | solution.py:30
  422.8 6.6 copy.11
  429.5 131.3 %reduce-scatter.8.cloned.1.call-done = f32[256,128]{1,0:T(8,128)} async-done(((f32[4096,128]{1,0:T(8,128)}), f32[256,128]{1,0:T(8,128)}) %reduce-scatter.8.cloned.1.call-update) | async-done | bytes 131088 | tf_op jit(solution)/shard_map/reduce_scatter | solution.py:92
  565.2 67.1 %reduce-scatter.6.cloned.1.call-done = f32[256,256]{1,0:T(8,128)} async-done(((f32[4096,256]{1,0:T(8,128)}), f32[256,256]{1,0:T(8,128)}) %reduce-scatter.6.cloned.1.call-update) | async-done | bytes 262160 | tf_op jit(solution)/shard_map/reduce_scatter | solution.py:79
  634.2 254.5 %all-reduce.3.cloned.1.call-done = (f32[256,256]{1,0:T(8,128)}, f32[256,128]{1,0:T(8,128)}) async-done(((f32[256,256]{1,0:T(8,128)}, f32[256,128]{1,0:T(8,128)}), (f32[256,256]{1,0:T(8,128)}, f32[256,128]{1,0:T(8,128)})) %all-reduce.3.cloned.1.call-update) | async-done | bytes 393232 | tf_op jit(solution)/shard_map/psum | solution.py:100
  (113 shorter events, 83.8 us)
Async XLA Ops:
  7.2 226.8 %copy-start = (bf16[256,256]{1,0:T(8,128)(2,1)S(1)}, bf16[256,256]{1,0:T(8,128)(2,1)}, u32[]{:S(2)}) copy-start(bf16[256,256]{1,0:T(8,128)(2,1)} %param.19) | copy-start | bytes 393220
  7.2 89.2 %all-gather.4.cloned.1.call-start = ((), (), s32[]{:S(2)}) async-start(), calls=%async_computation.3 | async-start | bytes 2228224 | tf_op jit(solution)/shard_map/all_gather | solution.py:55
  7.9 226.1 %reduce-scatter.4.cloned.1.call-start = ((), (), s32[]{:S(2)}) async-start(), calls=%async_computation.4 | async-start | bytes 4456448 | tf_op jit(solution)/shard_map/reduce_scatter | solution.py:65
  167.7 105.5 %all-gather.8.cloned.1.call-start = ((), (), s32[]{:S(2)}) async-start(), calls=%async_computation.7 | async-start | bytes 1114112 | tf_op jit(solution)/shard_map/all_gather | solution.py:82
  168.4 189.4 %all-gather.6.cloned.1.call-start = ((), (), s32[]{:S(2)}) async-start(), calls=%async_computation.5 | async-start | bytes 2228224 | tf_op jit(solution)/shard_map/all_gather | solution.py:69
  235.9 324.9 %reduce-scatter.8.cloned.1.call-start = ((), (), s32[]{:S(2)}) async-start(), calls=%async_computation.8 | async-start | bytes 2228224 | tf_op jit(solution)/shard_map/reduce_scatter | solution.py:92
  313.0 319.3 %reduce-scatter.6.cloned.1.call-start = ((), (), s32[]{:S(2)}) async-start(), calls=%async_computation.6 | async-start | bytes 4456448 | tf_op jit(solution)/shard_map/reduce_scatter | solution.py:79
  429.4 131.4 %copy-start.1 = (bf16[256,256]{1,0:T(8,128)(2,1)S(1)}, bf16[256,256]{1,0:T(8,128)(2,1)}, u32[]{:S(2)}) copy-start(bf16[256,256]{1,0:T(8,128)(2,1)} %get-tuple-element.261) | copy-start | bytes 393220
  429.4 133.3 %copy-start.3 = (bf16[256,128]{1,0:T(8,128)(2,1)S(1)}, bf16[256,128]{1,0:T(8,128)(2,1)}, u32[]{:S(2)}) copy-start(bf16[256,128]{1,0:T(8,128)(2,1)} %param.20) | copy-start | bytes 196612
  429.4 134.5 %copy-start.2 = (f32[256,256]{1,0:T(8,128)S(1)}, f32[256,256]{1,0:T(8,128)}, u32[]{:S(2)}) copy-start(f32[256,256]{1,0:T(8,128)} %reduce-scatter.4.cloned.1.call-done) | copy-start | bytes 786436
  429.4 459.3 %all-reduce.3.cloned.1.call-start = ((), (), s32[]{:S(2)}) async-start(), calls=%async_computation.9 | async-start | bytes 786432 | tf_op jit(solution)/shard_map/psum | solution.py:100
Sparse Core Ops, SparseCore 0:
  10.6 85.6 all-gather.3
  167.8 66.1 reduce-scatter.3
  235.9 37.2 all-gather.7
  276.2 81.5 all-gather.5
  361.5 199.2 reduce-scatter.7
  563.2 69.0 reduce-scatter.5
  638.4 250.2 all-reduce.2
where the time goes:
time: 900 us; the launch traced here: 899 us
  waiting for transfers between devices  688 us (76%)
  matrix products  147 us (16%)
  local copies, waits for them, and re-layouts  47.9 us (5%)
  between operations  14.8 us (2%)
    psum x1, waiting for transfers between devices, on_device(): first_grad = lax.psum(first_local, ('row', 'col'))  255 us
    reduce_scatter x1, waiting for transfers between devices, on_device(): lax.psum_scatter(grad_part, 'col', scatter_dimension=0, tiled=True)  131 us
    dot_general x12, matrix products, add_group(): jnp.einsum('tr,taw->raw', select, products, precision=HIGHEST)  99.3 us
    all_gather x1, waiting for transfers between devices, on_device(): gathered_x = lax.all_gather(node_features, 'col', axis=0, tiled=True)  86.8 us
    reduce_scatter x1, waiting for transfers between devices, on_device(): lax.psum_scatter(hidden_part, 'row', scatter_dimension=0, tiled=True)  67.1 us
    reduce_scatter x1, waiting for transfers between devices, on_device(): lax.psum_scatter(feature_part, 'row', scatter_dimension=0, tiled=True)  65.5 us
    all_gather x1, waiting for transfers between devices, on_device(): gathered_h = lax.all_gather(hidden_act, 'col', axis=0, tiled=True)  44.8 us
    dot_general x12, matrix products, add_group(): jnp.einsum(einsum_form, group_tiles, picked, preferred_element_type=jnp.f...  39.1 us
  transfers between devices with their start and end apart: 7, of which 7 were waited for; matrix products, arithmetic and copies ran while one was open for 13% of the time, Pallas kernels for 0%

commit v1 on v0

--- a/solution.py
+++ b/solution.py
@@ -97,7 +97,7 @@
     pre_grad = hidden_grad * (sigma * (1.0 + first_pre * (1.0 - sigma)))
     second_grad = lax.psum(second_local, ("row", "col"))
     first_local = jnp.dot(first_mean.T, pre_grad, precision=HIGHEST) * scale
-    first_grad = lax.psum(first_local, ("row", "col"))
+    first_grad = lax.psum(lax.psum(first_local, "col"), "row")
     return (output, first_grad, second_grad)
 
 

time: 900 us -> 1130 us (1.26)
  waiting for transfers between devices: 688 us -> 922 us
    psum x1 -> x3, waiting for transfers between devices: 255 us -> 446 us  [the longest x1 248 us: on_device(): second_grad = lax.psum(second_local, ('row', 'col'))]
    reduce_scatter x1, waiting for transfers between devices: 131 us -> 203 us  [on_device(): lax.psum_scatter(grad_part, 'col', scatter_dimension=0, tiled=True)]
    reduce_scatter x1, waiting for transfers between devices: 65.5 us -> 25.9 us  [on_device(): lax.psum_scatter(feature_part, 'row', scatter_dimension=0, tiled=True)]
    all_gather x1, waiting for transfers between devices: 44.8 us -> 84.3 us  [on_device(): gathered_h = lax.all_gather(hidden_act, 'col', axis=0, tiled=True)]
    all_gather x1, waiting for transfers between devices: 37 us -> 0.02 us  [on_device(): gathered_g = lax.all_gather(out_grad, 'row', axis=0, tiled=True)]
  transfers between devices with their start and end apart: 7 -> 9, of which waited for: 7 -> 8; matrix products, arithmetic and copies ran while one was open for 13% -> 17% of each run, Pallas kernels for 0% -> 0%
where the time goes in v1:
time: 1130 us
  waiting for transfers between devices  922 us (82%)
  matrix products  146 us (13%)
  local copies, waits for them, and re-layouts  48.7 us (4%)
  between operations  14.6 us (1%)
    psum x1, waiting for transfers between devices, on_device(): second_grad = lax.psum(second_local, ('row', 'col'))  248 us
    reduce_scatter x1, waiting for transfers between devices, on_device(): lax.psum_scatter(grad_part, 'col', scatter_dimension=0, tiled=True)  203 us
    psum x2, waiting for transfers between devices, on_device(): first_grad = lax.psum(lax.psum(first_local, 'col'), 'row')  198 us
    dot_general x12, matrix products, add_group(): jnp.einsum('tr,taw->raw', select, products, precision=HIGHEST)  99.2 us
    all_gather x1, waiting for transfers between devices, on_device(): gathered_x = lax.all_gather(node_features, 'col', axis=0, tiled=True)  86 us
    all_gather x1, waiting for transfers between devices, on_device(): gathered_h = lax.all_gather(hidden_act, 'col', axis=0, tiled=True)  84.3 us
    reduce_scatter x1, waiting for transfers between devices, on_device(): lax.psum_scatter(hidden_part, 'row', scatter_dimension=0, tiled=True)  75.7 us
    dot_general x12, matrix products, add_group(): jnp.einsum(einsum_form, group_tiles, picked, preferred_element_type=jnp.f...  38.9 us
  transfers between devices with their start and end apart: 9, of which 8 were waited for; matrix products, arithmetic and copies ran while one was open for 17% of the time, Pallas kernels for 0%

profile of v1, /device:TPU:1, one launch (start us, length us, event | category | flops | bytes accessed | tf_op | source)
XLA Modules:
  0.0 1133.1 jit_solution(2484465045678664248)
XLA Ops:
  10.3 86.0 %all-gather.4.cloned.1.call-done = bf16[4096,256]{1,0:T(8,128)(2,1)} async-done(((bf16[256,256]{1,0:T(8,128)(2,1)}), bf16[4096,256]{1,0:T(8,128)(2,1)}) %all-gather.4.cloned.1.call-update) | async-done | bytes 2097168 | tf_op jit(solution)/shard_map/all_gather | solution.py:55
  96.3 64.6 %while.33 = (s32[]{:T(128)}, f32[32,128,256]{2,0,1:T(8,128)}, s32[4,32]{1,0:T(4,128)S(1)}, pred[4,32]{1,0:T(4,128)(4,1)S(1)}, bf16[4,32,128,128]{3,2,1,0:T(8,128...) while((s32[]{:T(128)}, f32[32,128,256]{2,0,1:T(8,128)}, ...), condition=%wide.region_1.3_spmd.clone, body=%wide.region_0.2_spmd.clone.sunk | while | flops 674237632 | bytes 24123028 | solution.py:34
  102.6 8.9 select_add_fusion.6
  117.8 10.2 select_add_fusion.6
  134.3 10.2 select_add_fusion.6
  150.8 10.2 select_add_fusion.6
  161.0 6.6 copy.10
  167.8 35.7 %while.35 = (s32[]{:T(128)}, f32[32,128,128]{2,0,1:T(8,128)}, s32[4,32]{1,0:T(4,128)S(1)}, pred[4,32]{1,0:T(4,128)(4,1)S(1)}, bf16[4,32,128,128]{3,2,1,0:T(8,128...) while((s32[]{:T(128)}, f32[32,128,128]{2,0,1:T(8,128)}, ...), condition=%wide.region_7.9_spmd.clone, body=%wide.region_6.8_spmd.clone.sunk | while | flops 337120544 | bytes 12588823 | solution.py:34
  179.4 5.5 select_add_fusion.8
  188.8 5.5 select_add_fusion.8
  198.1 5.4 select_add_fusion.8
  207.8 25.9 %reduce-scatter.4.cloned.1.call-done = f32[256,256]{1,0:T(8,128)} async-done(((f32[4096,256]{1,0:T(8,128)}), f32[256,256]{1,0:T(8,128)}) %reduce-scatter.4.cloned.1.call-update) | async-done | bytes 262160 | tf_op jit(solution)/shard_map/reduce_scatter | solution.py:65
  235.8 202.9 %reduce-scatter.8.cloned.1.call-done = f32[256,128]{1,0:T(8,128)} async-done(((f32[4096,128]{1,0:T(8,128)}), f32[256,128]{1,0:T(8,128)}) %reduce-scatter.8.cloned.1.call-update) | async-done | bytes 131088 | tf_op jit(solution)/shard_map/reduce_scatter | solution.py:92
  442.4 84.3 %all-gather.6.cloned.1.call-done = bf16[4096,256]{1,0:T(8,128)(2,1)} async-done(((bf16[256,256]{1,0:T(8,128)(2,1)}), bf16[4096,256]{1,0:T(8,128)(2,1)}) %all-gather.6.cloned.1.call-update) | async-done | bytes 2097168 | tf_op jit(solution)/shard_map/all_gather | solution.py:69
  526.7 64.7 %while.34 = (s32[]{:T(128)}, f32[32,128,256]{2,0,1:T(8,128)}, s32[4,32]{1,0:T(4,128)S(1)}, pred[4,32]{1,0:T(4,128)(4,1)S(1)}, bf16[4,32,128,128]{3,2,1,0:T(8,128...) while((s32[]{:T(128)}, f32[32,128,256]{2,0,1:T(8,128)}, ...), condition=%wide.region_4.6_spmd.clone, body=%wide.region_3.5_spmd.clone.sunk | while | flops 674237632 | bytes 24123028 | solution.py:34
  533.0 8.9 select_add_fusion.7
  548.2 10.2 select_add_fusion.7
  564.7 10.2 select_add_fusion.7
  581.2 10.2 select_add_fusion.7
  591.4 6.6 copy.11
  600.0 75.7 %all-reduce.4.cloned.1.call-done = f32[256,256]{1,0:T(8,128)} async-done(((f32[256,256]{1,0:T(8,128)}), f32[256,256]{1,0:T(8,128)}) %all-reduce.4.cloned.1.call-update) | async-done | bytes 262160 | tf_op jit(solution)/shard_map/psum | solution.py:100
  675.8 75.7 %reduce-scatter.6.cloned.1.call-done = f32[256,256]{1,0:T(8,128)} async-done(((f32[4096,256]{1,0:T(8,128)}), f32[256,256]{1,0:T(8,128)}) %reduce-scatter.6.cloned.1.call-update) | async-done | bytes 262160 | tf_op jit(solution)/shard_map/reduce_scatter | solution.py:79
  753.3 248.0 %all-reduce.8.cloned.1.call-done = f32[256,128]{1,0:T(8,128)} async-done(((f32[256,128]{1,0:T(8,128)}), f32[256,128]{1,0:T(8,128)}) %all-reduce.8.cloned.1.call-update) | async-done | bytes 131088 | tf_op jit(solution)/shard_map/psum | solution.py:98
  1001.3 122.0 %all-reduce.6.cloned.1.call-done = f32[256,256]{1,0:T(8,128)} async-done(((f32[256,256]{1,0:T(8,128)}), f32[256,256]{1,0:T(8,128)}) %all-reduce.6.cloned.1.call-update) | async-done | bytes 262160 | tf_op jit(solution)/shard_map/psum | solution.py:100
  (119 shorter events, 89.0 us)
Async XLA Ops:
  7.2 226.6 %copy-start = (bf16[256,256]{1,0:T(8,128)(2,1)S(1)}, bf16[256,256]{1,0:T(8,128)(2,1)}, u32[]{:S(2)}) copy-start(bf16[256,256]{1,0:T(8,128)(2,1)} %param.19) | copy-start | bytes 393220
  7.2 89.2 %all-gather.4.cloned.1.call-start = ((), (), s32[]{:S(2)}) async-start(), calls=%async_computation.3 | async-start | bytes 2228224 | tf_op jit(solution)/shard_map/all_gather | solution.py:55
  7.9 159.9 %all-gather.8.cloned.1.call-start = ((), (), s32[]{:S(2)}) async-start(), calls=%async_computation.7 | async-start | bytes 1114112 | tf_op jit(solution)/shard_map/all_gather | solution.py:82
  8.7 225.1 %reduce-scatter.4.cloned.1.call-start = ((), (), s32[]{:S(2)}) async-start(), calls=%async_computation.4 | async-start | bytes 4456448 | tf_op jit(solution)/shard_map/reduce_scatter | solution.py:65
  167.6 271.1 %reduce-scatter.8.cloned.1.call-start = ((), (), s32[]{:S(2)}) async-start(), calls=%async_computation.8 | async-start | bytes 2228224 | tf_op jit(solution)/shard_map/reduce_scatter | solution.py:92
  203.6 235.1 %copy-start.3 = (bf16[256,128]{1,0:T(8,128)(2,1)S(1)}, bf16[256,128]{1,0:T(8,128)(2,1)}, u32[]{:S(2)}) copy-start(bf16[256,128]{1,0:T(8,128)(2,1)} %param.20) | copy-start | bytes 196612
  207.8 318.9 %all-gather.6.cloned.1.call-start = ((), (), s32[]{:S(2)}) async-start(), calls=%async_computation.5 | async-start | bytes 2228224 | tf_op jit(solution)/shard_map/all_gather | solution.py:69
  235.7 440.0 %all-reduce.4.cloned.1.call-start = ((), (), s32[]{:S(2)}) async-start(), calls=%async_computation.9 | async-start | bytes 524288 | tf_op jit(solution)/shard_map/psum | solution.py:100
  442.1 309.3 %reduce-scatter.6.cloned.1.call-start = ((), (), s32[]{:S(2)}) async-start(), calls=%async_computation.6 | async-start | bytes 4456448 | tf_op jit(solution)/shard_map/reduce_scatter | solution.py:79
  598.0 0.9 copy-start.1
  598.0 1.0 copy-start.2
  598.0 403.3 %all-reduce.8.cloned.1.call-start = ((), (), s32[]{:S(2)}) async-start(), calls=%async_computation.11 | async-start | bytes 262144 | tf_op jit(solution)/shard_map/psum | solution.py:98
  599.9 523.4 %all-reduce.6.cloned.1.call-start = ((), (), s32[]{:S(2)}) async-start(), calls=%async_computation.10 | async-start | bytes 524288 | tf_op jit(solution)/shard_map/psum | solution.py:100
Sparse Core Ops, SparseCore 0:
  10.6 85.6 all-gather.3
  98.2 35.5 all-gather.7
  167.7 66.0 reduce-scatter.3
  237.5 201.1 reduce-scatter.7
  441.7 85.0 all-gather.5
  529.8 145.9 all-reduce.3
  678.4 72.9 reduce-scatter.5
  758.4 242.8 all-reduce.7
  1004.1 119.1 all-reduce.5
